TPU v7x, 32 devices: a whole 2x2x4 slice. The times are simulated.
32 devices in a mesh: scan: 2 (over x), seq: 16 (over z, y, core).
Axes of the slice: x: 2, y: 2, z: 4, core: 2. Of those that a mesh axis runs over, the one named last changes fastest.
Arguments:
- tokens: bfloat16 [8192, 1024], P(('scan', 'seq')), parts along dimension 0, may hold values from -12 to 12
- ln_gain: float32 [1024], replicated, may hold values from 0.1 to 1.9
- w_query: bfloat16 [1024, 1024], P('seq'), may hold values from -2 to 2
- w_key: bfloat16 [1024, 1024], P('seq'), may hold values from -2 to 2
- w_value: bfloat16 [1024, 1024], P('seq'), may hold values from -0.1875 to 0.1875
- w_out: bfloat16 [1024, 1024], P('seq'), may hold values from -0.1875 to 0.1875
- probe_gain: float32 [1024], replicated, may hold values from 0.1 to 1.9
- probe_queries: bfloat16 [256, 1024], replicated, may hold values from -46 to 46
- key_blocks: int32 [64, 8], P('scan'), parts along dimension 0, may hold values from 0 to 31, as said below
- key_counts: int32 [64], P('scan'), parts along dimension 0, may hold values from 1 to 8, as said below
Outputs:
- layer_out: bfloat16 [8192, 1024], P(('scan', 'seq')), parts along dimension 0
- probe_out: float32 [512, 1024], P(('scan', 'seq')), parts along dimension 0
There are 2 independent parts, one for each index of `scan`. A program takes and returns all parts, laid end to end along the dimension named above; an argument that names none is the same for every part. Nothing has to cross between parts.
Inputs may be any that keep to these rules, and one draw needn't show every extreme that they name: `key_blocks`: entry 0 of each query block's list is that block itself; the entries of one list are different blocks. Entries at or after key_counts are ignored. `key_counts`: some block uses all 8 entries in every draw.
All inputs are finite; a program needn't handle non-finite values.
Results may differ from a plain program's by a relative error of at most 0.0061.
Values may be sent and summed in bfloat16 or wider, within the bound.
No kernel may reach another device: no remote copies, remote signals or barrier semaphores. Data moves between devices by JAX's collectives and lax.ppermute only.
A program may use at most 64 MiB of HBM per device.

v0:
```python
import math
import jax
import jax.numpy as jnp
from jax import lax
from jax.sharding import PartitionSpec as P

D = 1024
HEADS = 16
HEAD_DIM = 64
PROBES = 256
BLOCK = 128
MAXK = 8
TOK_DEV = 256
EPS = 1e-05


def layer_norm(values, gain):
    wide = values.astype(jnp.float32)
    center = wide - jnp.mean(wide, axis=-1, keepdims=True)
    spread = jnp.mean(center * center, axis=-1, keepdims=True)
    return (center * lax.rsqrt(spread + EPS) * gain).astype(jnp.bfloat16)


def widen_heads(factor):
    return jnp.repeat(jnp.transpose(factor), HEAD_DIM, axis=1)


def per_device(
    tokens,
    ln_gain,
    w_query,
    w_key,
    w_value,
    w_out,
    probe_gain,
    probe_queries,
    key_blocks,
    key_counts,
):
    scale = 1.0 / math.sqrt(HEAD_DIM)
    ranks = lax.axis_size("seq")
    group = ranks // HEADS
    piece_rows = TOK_DEV // group
    myself = lax.axis_index("seq")
    quarter = myself % group
    normed = layer_norm(tokens, ln_gain)
    columns = normed
    query = jnp.dot(
        columns,
        lax.all_gather(w_query, "seq", axis=0, tiled=True),
        preferred_element_type=jnp.float32,
    )
    keys = jnp.dot(
        columns,
        lax.all_gather(w_key, "seq", axis=0, tiled=True),
        preferred_element_type=jnp.float32,
    )
    values = jnp.dot(
        columns,
        lax.all_gather(w_value, "seq", axis=0, tiled=True),
        preferred_element_type=jnp.float32,
    )
    query = query.astype(jnp.bfloat16)
    pairs = jnp.concatenate(
        [
            keys.astype(jnp.bfloat16).reshape(TOK_DEV, HEADS, HEAD_DIM),
            values.astype(jnp.bfloat16).reshape(TOK_DEV, HEADS, HEAD_DIM),
        ],
        axis=2,
    )
    query_send = jnp.transpose(
        query.reshape(group, piece_rows, HEADS, HEAD_DIM), (2, 0, 1, 3)
    ).reshape(ranks, piece_rows * HEAD_DIM)
    pair_send = jnp.repeat(
        jnp.transpose(pairs, (1, 0, 2)).reshape(HEADS, TOK_DEV * 2 * HEAD_DIM), group, axis=0
    )
    query_got, pair_got = (
        lax.all_to_all(query_send, "seq", split_axis=0, concat_axis=0, tiled=True),
        lax.all_to_all(pair_send, "seq", split_axis=0, concat_axis=0, tiled=True),
    )
    pair_all = pair_got.reshape(ranks * TOK_DEV, 2 * HEAD_DIM)
    blocks_total = ranks * TOK_DEV // BLOCK
    pair_grid = pair_all.reshape(blocks_total, BLOCK, 2 * HEAD_DIM)
    unit = min(piece_rows, BLOCK)
    per_piece = piece_rows // unit
    units = ranks * per_piece
    unit_ids = jnp.arange(units, dtype=jnp.int32)
    starts = unit_ids // per_piece * TOK_DEV + quarter * piece_rows + unit_ids % per_piece * unit
    block_ids = starts // BLOCK
    unit_lists = key_blocks[block_ids]
    unit_counts = key_counts[block_ids]
    per_batch = min(units, max(1, 1024 // unit))
    batches = units // per_batch
    query_units = query_got.reshape(batches, per_batch, unit, HEAD_DIM)
    slot_of = jnp.arange(MAXK * BLOCK, dtype=jnp.int32) // BLOCK

    def attend_batch(operands):
        batch_query, batch_lists, batch_counts = operands
        picked = pair_grid[batch_lists].reshape(per_batch, MAXK * BLOCK, 2 * HEAD_DIM)
        batch_keys = picked[:, :, :HEAD_DIM]
        batch_values = picked[:, :, HEAD_DIM:]
        scores = (
            jnp.einsum("uqd,ukd->uqk", batch_query, batch_keys, preferred_element_type=jnp.float32)
            * scale
        )
        valid = slot_of[None, :] < batch_counts[:, None]
        scores = jnp.where(valid[:, None, :], scores, -jnp.inf)
        top = jnp.max(scores, axis=-1, keepdims=True)
        weights = jnp.exp(scores - top)
        total = jnp.sum(weights, axis=-1, keepdims=True)
        mixed = jnp.einsum(
            "uqk,ukd->uqd",
            weights.astype(jnp.bfloat16),
            batch_values,
            preferred_element_type=jnp.float32,
        )
        return (mixed / total).astype(jnp.bfloat16)

    attended_heads = lax.map(
        attend_batch,
        (
            query_units,
            unit_lists.reshape(batches, per_batch, MAXK),
            unit_counts.reshape(batches, per_batch),
        ),
    )
    returned = lax.all_to_all(
        attended_heads.reshape(ranks, piece_rows * HEAD_DIM),
        "seq",
        split_axis=0,
        concat_axis=0,
        tiled=True,
    )
    attended = jnp.transpose(
        returned.reshape(HEADS, group, piece_rows, HEAD_DIM), (1, 2, 0, 3)
    ).reshape(TOK_DEV, D)
    columns = attended
    projected = jnp.dot(
        columns,
        lax.all_gather(w_out, "seq", axis=0, tiled=True),
        preferred_element_type=jnp.float32,
    )
    layer_out = (tokens.astype(jnp.float32) + projected).astype(jnp.bfloat16)
    pooled = layer_norm(layer_out, probe_gain)
    pooled_heads = pooled.reshape(TOK_DEV, HEADS, HEAD_DIM)
    probe_heads = probe_queries.reshape(PROBES, HEADS, HEAD_DIM)
    probe_scores = (
        jnp.einsum("phd,nhd->hpn", probe_heads, pooled_heads, preferred_element_type=jnp.float32)
        * scale
    )
    pooled_wide = pooled_heads.astype(jnp.float32)
    own_top = jnp.max(probe_scores, axis=-1)
    top = lax.pmax(own_top, "seq")
    weights = jnp.exp(probe_scores - top[:, :, None])
    own_total = jnp.sum(weights, axis=-1)
    own_acc = jnp.einsum(
        "hpn,nhd->phd", weights, pooled_wide, precision=lax.Precision.HIGHEST
    ).reshape(PROBES, D)
    total, accum = lax.psum((own_total, own_acc), "seq")
    probe_all = accum / widen_heads(total)
    share = PROBES // ranks
    probe_out = lax.dynamic_slice_in_dim(probe_all, myself * share, share, 0)
    return (layer_out, probe_out)


def solution(mesh):
    return jax.shard_map(
        per_device,
        mesh=mesh,
        in_specs=(
            P(("scan", "seq"), None),
            P(),
            P("seq", None),
            P("seq", None),
            P("seq", None),
            P("seq", None),
            P(),
            P(),
            P("scan", None),
            P("scan"),
        ),
        out_specs=(P(("scan", "seq"), None), P(("scan", "seq"), None)),
        check_vma=False,
    )
```

profile of v0, /device:TPU:0, one launch (start us, length us, event | category | flops | bytes accessed | tf_op | source)
XLA Modules:
  0.0 426.3 jit_solution(11318317714799748280)
XLA Ops:
  11.9 42.4 %all-gather.5.cloned.1.call-done = bf16[1024,1024]{1,0:T(8,128)(2,1)} async-done(((bf16[64,1024]{1,0:T(8,128)(2,1)}), bf16[1024,1024]{1,0:T(8,128)(2,1)}) %all-gather.5.cloned.1.call-update) | async-done | bytes 2097168 | tf_op jit(solution)/shard_map/all_gather | solution.py:50
  54.3 2.5 convolution_convert_fusion.2
  58.7 3.8 reduce.3
  63.8 4.8 %all-to-all-start = ((bf16[16,2,8192]{2,1,0:T(2,128)(2,1)}), bf16[16,2,8192]{2,1,0:T(2,128)(2,1)}, u32[]{:S(2)}, u32[]{:S(2)}) async-start(bf16[16,2,8192]{2,1,0:T(2,128)(2,1)} %reshape.298), calls=%async_computation | async-start | bytes 1048576 | tf_op jit(solution)/shard_map/all_to_all | solution.py:78
  68.5 30.6 %all-gather.7.cloned.1.call-done = bf16[1024,1024]{1,0:T(8,128)(2,1)} async-done(((bf16[64,1024]{1,0:T(8,128)(2,1)}), bf16[1024,1024]{1,0:T(8,128)(2,1)}) %all-gather.7.cloned.1.call-update) | async-done | bytes 2097168 | tf_op jit(solution)/shard_map/all_gather | solution.py:55
  99.1 2.4 convolution_convert_fusion.1
  101.7 39.8 %all-gather.9.cloned.1.call-done = bf16[1024,1024]{1,0:T(8,128)(2,1)} async-done(((bf16[64,1024]{1,0:T(8,128)(2,1)}), bf16[1024,1024]{1,0:T(8,128)(2,1)}) %all-gather.9.cloned.1.call-update) | async-done | bytes 2097168 | tf_op jit(solution)/shard_map/all_gather | solution.py:60
  141.5 2.4 convolution_convert_fusion
  145.4 7.2 %reduce.4 = bf16[16,32768]{1,0:T(8,128)(2,1)S(1)} reduce(bf16[16,1,32768]{2,1,0:T(2,128)(2,1)S(1)} %all_to_all.25, bf16[]{:T(256)} %broadcast.287), dimensions={1}, to_apply=%all_to_all.25.reduce_sub_computation | reduce | bytes 2097154 | tf_op jit(solution)/shard_map/all_to_all | solution.py:79
  154.2 3.7 all-to-all-start.1
  159.9 2.4 reshape.299
  162.3 3.3 reduce
  167.9 15.6 %all-to-all-done.1 = bf16[16,2,16384]{2,1,0:T(2,128)(2,1)S(1)} async-done(((bf16[16,2,16384]{2,1,0:T(2,128)(2,1)}), bf16[16,2,16384]{2,1,0:T(2,128)(2,1)S(1)}, u32[]{:S(2)}, u32[]{:S(2)}) %all-to-all-start.1) | async-done | bytes 1048608 | tf_op jit(solution)/shard_map/all_to_all | solution.py:79
  184.5 6.7 %reduce.1 = bf16[16,32768]{1,0:T(8,128)(2,1)S(1)} reduce(bf16[16,1,32768]{2,1,0:T(2,128)(2,1)S(1)} %reshape.301, bf16[]{:T(256)} %constant.115), dimensions={1}, to_apply=%all_to_all.21.reduce_sub_computation | reduce | bytes 2097154 | tf_op jit(solution)/shard_map/all_to_all | solution.py:79
  191.7 27.2 %while.11 = (s32[]{:T(128)}, bf16[4,8,128,64]{2,3,1,0:T(8,128)(2,1)}, s32[4,8]{1,0:T(4,128)S(1)}, bf16[4,8,128,64]{2,3,1,0:T(8,128)(2,1)}, s32[4,8,8]{2,1,0:T(8,...) while((s32[]{:T(128)}, bf16[4,8,128,64]{2,3,1,0:T(8,128)(2,1)}, s32[4,8]{1,0:T(4,128)S(1)}, ...), condition=%wide.region_5.6_spmd.clone, body=%wide.region_2.5_spmd.clone.sunk | while | flops 280116416 | bytes 21301940 | solution.py:119
  196.0 2.7 fusion.87
  199.9 1.8 fusion.85
  202.7 2.7 fusion.87
  206.6 1.8 fusion.85
  209.5 2.7 fusion.87
  216.3 2.7 fusion.87
  221.2 3.8 reduce.5
  226.3 8.5 %all-to-all-start.2 = ((bf16[16,2,8192]{2,1,0:T(2,128)(2,1)}), bf16[16,2,8192]{2,1,0:T(2,128)(2,1)S(1)}, u32[]{:S(2)}, u32[]{:S(2)}) async-start(bf16[16,2,8192]{2,1,0:T(2,128)(2,1)} %reshape.302), calls=%async_computation.2 | async-start | bytes 1048576 | tf_op jit(solution)/shard_map/all_to_all | solution.py:127
  235.0 14.2 %all-to-all-done.2 = bf16[16,2,8192]{2,1,0:T(2,128)(2,1)S(1)} async-done(((bf16[16,2,8192]{2,1,0:T(2,128)(2,1)}), bf16[16,2,8192]{2,1,0:T(2,128)(2,1)S(1)}, u32[]{:S(2)}, u32[]{:S(2)}) %all-to-all-start.2) | async-done | bytes 524320 | tf_op jit(solution)/shard_map/all_to_all | solution.py:127
  250.0 3.3 reduce.2
  254.9 2.4 convert_reduce_fusion.1
  258.1 2.7 bitcast_reduce_fusion
  260.8 60.1 %pmax.7 = f32[16,256]{1,0:T(8,128)S(1)} all-reduce(f32[16,256]{1,0:T(8,128)S(1)} %get-tuple-element.94), channel_id=1, replica_groups=mesh['scan'=2,'seq'=16] {'seq'}, use_global_device_ids=true, to_apply=%region_9.10 | all-reduce | flops 4096 | bytes 32768 | tf_op jit(solution)/shard_map/pmax | solution.py:153
  320.9 5.4 %fusion.45 = f32[16,64,256]{2,1,0:T(8,128)} fusion(bf16[256,16,64]{0,2,1:T(8,128)(2,1)S(1)} %bitcast.70, f32[16,256,256]{2,1,0:T(8,128)} %get-tuple-element.95, f32[16,256]{1,0:T(8,128)S(1)} %pmax.7), kind=kOutput, calls=%fused_computation.42 | convolution fusion | flops 807403520 | bytes 5783552 | tf_op jit(solution)/shard_map/hpn,nhd->phd/dot_general | solution.py:156
  326.4 2.9 fusion.44
  329.3 58.1 %psum.15 = f32[256,16]{0,1:T(8,128)S(1)} all-reduce(f32[256,16]{0,1:T(8,128)S(1)} %bitcast.80), channel_id=1, replica_groups=mesh['scan'=2,'seq'=16] {'seq'}, use_global_device_ids=true, to_apply=%region_12.13 | all-reduce | flops 4096 | bytes 32768 | tf_op jit(solution)/shard_map/psum | solution.py:159
  387.4 29.6 %all-reduce.2.cloned.1.call-done = f32[256,1024]{0,1:T(8,128)} async-done(((f32[256,1024]{0,1:T(8,128)}), f32[256,1024]{0,1:T(8,128)}) %all-reduce.2.cloned.1.call-update) | async-done | bytes 1048592 | tf_op jit(solution)/shard_map/psum | solution.py:159
  (103 shorter events, 38.4 us)
Async XLA Ops:
  7.2 152.0 %copy-start = (s32[32]{0:T(128)S(1)}, s32[32]{0:T(128)}, u32[]{:S(2)}) copy-start(s32[32]{0:T(128)} %param.21) | copy-start | bytes 388
  7.2 47.1 %all-gather.5.cloned.1.call-start = ((), (), s32[]{:S(2)}) async-start(), calls=%async_computation.3 | async-start | bytes 2228224 | tf_op jit(solution)/shard_map/all_gather | solution.py:50
  7.9 91.2 %all-gather.7.cloned.1.call-start = ((), (), s32[]{:S(2)}) async-start(), calls=%async_computation.4 | async-start | bytes 2228224 | tf_op jit(solution)/shard_map/all_gather | solution.py:55
  8.7 132.8 %all-gather.9.cloned.1.call-start = ((), (), s32[]{:S(2)}) async-start(), calls=%async_computation.5 | async-start | bytes 2228224 | tf_op jit(solution)/shard_map/all_gather | solution.py:60
  56.9 42.3 %copy-start.1 = (bf16[256,1024]{1,0:T(8,128)(2,1)S(1)}, bf16[256,1024]{1,0:T(8,128)(2,1)}, u32[]{:S(2)}) copy-start(bf16[256,1024]{1,0:T(8,128)(2,1)} %param.12) | copy-start | bytes 1572868
  56.9 42.3 %copy-start.7 = (f32[1024]{0:T(1024)S(1)}, f32[1024]{0:T(1024)}, u32[]{:S(2)}) copy-start(f32[1024]{0:T(1024)} %param.13) | copy-start | bytes 12292
  63.8 90.4 %all-to-all-start = ((bf16[16,2,8192]{2,1,0:T(2,128)(2,1)}), bf16[16,2,8192]{2,1,0:T(2,128)(2,1)}, u32[]{:S(2)}, u32[]{:S(2)}) async-start(bf16[16,2,8192]{2,1,0:T(2,128)(2,1)} %reshape.298), calls=%async_computation | async-start | bytes 1048576 | tf_op jit(solution)/shard_map/all_to_all | solution.py:78
  145.3 13.1 %copy-start.6 = (s32[32,8]{0,1:T(8,128)S(1)}, s32[32,8]{0,1:T(8,128)}, u32[]{:S(2)}) copy-start(s32[32,8]{0,1:T(8,128)} %param.20) | copy-start | bytes 3076
  154.2 29.3 %all-to-all-start.1 = ((bf16[16,2,16384]{2,1,0:T(2,128)(2,1)}), bf16[16,2,16384]{2,1,0:T(2,128)(2,1)S(1)}, u32[]{:S(2)}, u32[]{:S(2)}) async-start(bf16[16,2,16384]{2,1,0:T(2,128)(2,1)} %reshape.300), calls=%async_computation.1 | async-start | bytes 2097152 | tf_op jit(solution)/shard_map/all_to_all | solution.py:79
  157.9 97.0 %all-gather.11.cloned.1.call-start = ((), (), s32[]{:S(2)}) async-start(), calls=%async_computation.6 | async-start | bytes 2228224 | tf_op jit(solution)/shard_map/all_gather | solution.py:140
  219.0 15.9 %copy-start.4 = (bf16[256,1024]{1,0:T(8,128)(2,1)S(1)}, bf16[256,1024]{1,0:T(8,128)(2,1)}, u32[]{:S(2)}) copy-start(bf16[256,1024]{1,0:T(8,128)(2,1)} %param.19) | copy-start | bytes 1572868
  226.3 28.6 %copy-start.2 = (bf16[256,1024]{1,0:T(8,128)(2,1)S(1)}, bf16[256,1024]{1,0:T(8,128)(2,1)}, u32[]{:S(2)}) copy-start(bf16[256,1024]{1,0:T(8,128)(2,1)} %param.12) | copy-start | bytes 1572868
  226.3 23.0 %all-to-all-start.2 = ((bf16[16,2,8192]{2,1,0:T(2,128)(2,1)}), bf16[16,2,8192]{2,1,0:T(2,128)(2,1)S(1)}, u32[]{:S(2)}, u32[]{:S(2)}) async-start(bf16[16,2,8192]{2,1,0:T(2,128)(2,1)} %reshape.302), calls=%async_computation.2 | async-start | bytes 1048576 | tf_op jit(solution)/shard_map/all_to_all | solution.py:127
  234.8 182.3 %all-reduce.2.cloned.1.call-start = ((), (), s32[]{:S(2)}) async-start(), calls=%async_computation.7 | async-start | bytes 2097152 | tf_op jit(solution)/shard_map/psum | solution.py:159
  250.0 7.6 %copy-start.5 = (f32[1024]{0:T(1024)S(1)}, f32[1024]{0:T(1024)}, u32[]{:S(2)}) copy-start(f32[1024]{0:T(1024)} %param.18) | copy-start | bytes 12292
  257.3 69.1 %copy-start.3 = (bf16[256,1024]{1,0:T(8,128)(2,1)}, bf16[256,1024]{1,0:T(8,128)(2,1)S(1)}, u32[]{:S(2)}) copy-start(bf16[256,1024]{1,0:T(8,128)(2,1)S(1)} %get-tuple-element.93) | copy-start | bytes 1572868
Sparse Core Ops, SparseCore 0:
  10.2 44.0 all-gather.4
  56.5 42.6 all-gather.6
  101.3 40.1 all-gather.8
  160.6 48.5 all-gather.10
  326.5 90.4 all-reduce.1
where the time goes:
time: 432 us; the launch traced here: 426 us
  waiting for transfers between devices  175 us (41%)
  blocking collectives  118 us (27%)
  other arithmetic  40.5 us (9%)
  matrix products  35.7 us (8%)
  local copies, waits for them, and re-layouts  25 us (6%)
  starting transfers between devices  17.1 us (4%)
  between operations  14.6 us (3%)
    pmax x1, blocking collectives, per_device(): top = lax.pmax(own_top, 'seq')  60.1 us
    psum x1, blocking collectives, per_device(): total, accum = lax.psum((own_total, own_acc), 'seq')  58.1 us
    all_gather x1, waiting for transfers between devices, per_device(): lax.all_gather(w_query, 'seq', axis=0, tiled=True)  42.4 us
    all_gather x1, waiting for transfers between devices, per_device(): lax.all_gather(w_value, 'seq', axis=0, tiled=True)  39.8 us
    all_gather x1, waiting for transfers between devices, per_device(): lax.all_gather(w_key, 'seq', axis=0, tiled=True)  30.6 us
    psum x1, waiting for transfers between devices, per_device(): total, accum = lax.psum((own_total, own_acc), 'seq')  29.6 us
    all_to_all x1, waiting for transfers between devices, per_device(): lax.all_to_all(pair_send, 'seq', split_axis=0, concat_axis=0, tiled=True)  15.6 us
    all_to_all x1, waiting for transfers between devices, per_device(): lax.all_to_all(attended_heads.reshape(ranks, piece_rows * HEAD_DIM), 'seq...  14.2 us
  transfers between devices with their start and end apart: 8, of which 6 were waited for; matrix products, arithmetic and copies ran while one was open for 20% of the time, Pallas kernels for 0%

commit v1 on v0

--- a/solution.py
+++ b/solution.py
@@ -1,3 +1,4 @@
+import functools
 import math
 import jax
 import jax.numpy as jnp
@@ -12,6 +13,39 @@
 MAXK = 8
 TOK_DEV = 256
 EPS = 1e-05
+
+
+def direct_state(panel, at_axis, vec):
+    near = panel.shape
+    return jnp.moveaxis(
+        panel.reshape(*near[:at_axis], vec, near[at_axis] // vec, *near[at_axis + 1 :]), at_axis, 0
+    )
+
+
+def settle_sides(target, which_dim):
+    target = jnp.moveaxis(target, 0, which_dim)
+    val = target.shape
+    return target.reshape(
+        *val[:which_dim], val[which_dim] * val[which_dim + 1], *val[which_dim + 2 :]
+    )
+
+
+def results_name(block_in, row_axis, local_array, tile_in):
+    passed, reply = (lax.axis_size(row_axis), lax.axis_index(row_axis))
+    current_arr = direct_state(block_in, local_array, passed)
+    odd = current_arr
+    for s in range(1, passed):
+        local_now, z1 = ((reply + s) % passed, (reply - s) % passed)
+        later = lax.dynamic_index_in_dim(current_arr, local_now, 0)
+        sheets = []
+        for b in range(passed):
+            sheets.append((b, (b + s) % passed))
+        all_rows = lax.ppermute(later, row_axis, perm=sheets)
+        odd = lax.dynamic_update_slice_in_dim(odd, all_rows, z1, axis=0)
+    return settle_sides(odd, tile_in)
+
+
+trace_block_for = functools.partial(results_name, row_axis="seq", local_array=0, tile_in=0)
 
 
 def layer_norm(values, gain):
@@ -124,13 +158,7 @@
             unit_counts.reshape(batches, per_batch),
         ),
     )
-    returned = lax.all_to_all(
-        attended_heads.reshape(ranks, piece_rows * HEAD_DIM),
-        "seq",
-        split_axis=0,
-        concat_axis=0,
-        tiled=True,
-    )
+    returned = trace_block_for(attended_heads.reshape(ranks, piece_rows * HEAD_DIM))
     attended = jnp.transpose(
         returned.reshape(HEADS, group, piece_rows, HEAD_DIM), (1, 2, 0, 3)
     ).reshape(TOK_DEV, D)

time: 432 us -> 447 us (1.035)
  local copies, waits for them, and re-layouts: 25 us -> 41.8 us
  starting transfers between devices: 17.1 us -> 31.8 us
  waiting for transfers between devices: 175 us -> 168 us
  other arithmetic: 40.5 us -> 33.6 us
    ppermute x0 -> x15, starting transfers between devices: none -> 23.5 us  [results_name(): all_rows = lax.ppermute(later, row_axis, perm=sheets)]
    dynamic_update_slice x0 -> x15, local copies, waits for them, and re-layouts: none -> 17.3 us  [results_name(): odd = lax.dynamic_update_slice_in_dim(odd, all_rows, z1, axis=0)]
    all_to_all x1 -> x0, waiting for transfers between devices: 14.2 us -> none  [per_device(): lax.all_to_all(attended_heads.reshape(ranks, piece_rows * HEAD_DIM), 'seq...]
    all_gather x1, waiting for transfers between devices: 30.6 us -> 39.8 us  [per_device(): lax.all_gather(w_key, 'seq', axis=0, tiled=True)]
    all_gather x1, waiting for transfers between devices: 39.8 us -> 30.6 us  [per_device(): lax.all_gather(w_value, 'seq', axis=0, tiled=True)]
    all_to_all x1 -> x0, starting transfers between devices: 8.51 us -> none  [per_device(): lax.all_to_all(attended_heads.reshape(ranks, piece_rows * HEAD_DIM), 'seq...]
    ppermute x0 -> x15, waiting for transfers between devices: none -> 7.29 us  [results_name(): all_rows = lax.ppermute(later, row_axis, perm=sheets)]
    all_to_all x2 -> x0, other arithmetic: 7.15 us -> none  [per_device(): lax.all_to_all(attended_heads.reshape(ranks, piece_rows * HEAD_DIM), 'seq...]
  transfers between devices with their start and end apart: 8 -> 22, of which waited for: 6 -> 8; matrix products, arithmetic and copies ran while one was open for 20% -> 22% of each run, Pallas kernels for 0% -> 0%
where the time goes in v1:
time: 447 us; the launch traced here: 442 us
  waiting for transfers between devices  168 us (38%)
  blocking collectives  116 us (26%)
  local copies, waits for them, and re-layouts  41.8 us (9%)
  matrix products  35.7 us (8%)
  other arithmetic  33.6 us (8%)
  starting transfers between devices  31.8 us (7%)
  between operations  14.8 us (3%)
    psum x1, blocking collectives, per_device(): total, accum = lax.psum((own_total, own_acc), 'seq')  58.1 us
    pmax x1, blocking collectives, per_device(): top = lax.pmax(own_top, 'seq')  58 us
    all_gather x1, waiting for transfers between devices, per_device(): lax.all_gather(w_query, 'seq', axis=0, tiled=True)  42.4 us
    all_gather x1, waiting for transfers between devices, per_device(): lax.all_gather(w_key, 'seq', axis=0, tiled=True)  39.8 us
    all_gather x1, waiting for transfers between devices, per_device(): lax.all_gather(w_value, 'seq', axis=0, tiled=True)  30.6 us
    psum x1, waiting for transfers between devices, per_device(): total, accum = lax.psum((own_total, own_acc), 'seq')  29.7 us
    ppermute x15, starting transfers between devices, results_name(): all_rows = lax.ppermute(later, row_axis, perm=sheets)  23.5 us
    dynamic_update_slice x15, local copies, waits for them, and re-layouts, results_name(): odd = lax.dynamic_update_slice_in_dim(odd, all_rows, z1, axis=0)  17.3 us
  transfers between devices with their start and end apart: 22, of which 8 were waited for; matrix products, arithmetic and copies ran while one was open for 22% of the time, Pallas kernels for 0%

profile of v1, /device:TPU:0, one launch (start us, length us, event | category | flops | bytes accessed | tf_op | source)
XLA Modules:
  0.0 441.7 jit_solution(14808259195285282156)
XLA Ops:
  11.9 42.4 %all-gather.5.cloned.1.call-done = bf16[1024,1024]{1,0:T(8,128)(2,1)} async-done(((bf16[64,1024]{1,0:T(8,128)(2,1)}), bf16[1024,1024]{1,0:T(8,128)(2,1)}) %all-gather.5.cloned.1.call-update) | async-done | bytes 2097168 | tf_op jit(solution)/shard_map/all_gather | solution.py:84
  54.3 2.5 convolution_convert_fusion.2
  58.8 3.9 reduce.2
  63.9 4.4 all-to-all-start
  68.3 30.6 %all-gather.9.cloned.1.call-done = bf16[1024,1024]{1,0:T(8,128)(2,1)} async-done(((bf16[64,1024]{1,0:T(8,128)(2,1)}), bf16[1024,1024]{1,0:T(8,128)(2,1)}) %all-gather.9.cloned.1.call-update) | async-done | bytes 2097168 | tf_op jit(solution)/shard_map/all_gather | solution.py:94
  98.9 2.4 convolution_convert_fusion
  101.5 39.8 %all-gather.7.cloned.1.call-done = bf16[1024,1024]{1,0:T(8,128)(2,1)} async-done(((bf16[64,1024]{1,0:T(8,128)(2,1)}), bf16[1024,1024]{1,0:T(8,128)(2,1)}) %all-gather.7.cloned.1.call-update) | async-done | bytes 2097168 | tf_op jit(solution)/shard_map/all_gather | solution.py:89
  141.3 2.4 convolution_convert_fusion.1
  145.1 7.3 %reduce.3 = bf16[16,32768]{1,0:T(8,128)(2,1)S(1)} reduce(bf16[16,1,32768]{2,1,0:T(2,128)(2,1)S(1)} %all_to_all.17, bf16[]{:T(256)} %broadcast.316), dimensions={1}, to_apply=%all_to_all.17.reduce_sub_computation | reduce | bytes 2097154 | tf_op jit(solution)/shard_map/all_to_all | solution.py:113
  154.1 3.7 all-to-all-start.1
  160.1 2.4 reshape.289
  162.6 3.3 reduce
  168.1 15.2 %all-to-all-done.1 = bf16[16,2,16384]{2,1,0:T(2,128)(2,1)S(1)} async-done(((bf16[16,2,16384]{2,1,0:T(2,128)(2,1)}), bf16[16,2,16384]{2,1,0:T(2,128)(2,1)S(1)}, u32[]{:S(2)}, u32[]{:S(2)}) %all-to-all-start.1) | async-done | bytes 1048608 | tf_op jit(solution)/shard_map/all_to_all | solution.py:113
  184.4 6.7 %reduce.1 = bf16[16,32768]{1,0:T(8,128)(2,1)S(1)} reduce(bf16[16,1,32768]{2,1,0:T(2,128)(2,1)S(1)} %reshape.291, bf16[]{:T(256)} %constant.324), dimensions={1}, to_apply=%all_to_all.15.reduce_sub_computation | reduce | bytes 2097154 | tf_op jit(solution)/shard_map/all_to_all | solution.py:113
  191.6 27.4 %while.11 = (s32[]{:T(128)}, bf16[4,8,128,64]{2,3,1,0:T(8,128)(2,1)}, s32[4,8]{1,0:T(4,128)S(1)}, bf16[4,8,128,64]{2,3,1,0:T(8,128)(2,1)}, s32[4,8,8]{2,1,0:T(8,...) while((s32[]{:T(128)}, bf16[4,8,128,64]{2,3,1,0:T(8,128)(2,1)}, s32[4,8]{1,0:T(4,128)S(1)}, ...), condition=%wide.region_5.6_spmd.clone, body=%wide.region_2.5_spmd.clone.sunk | while | flops 280116416 | bytes 21300932 | solution.py:153
  196.1 2.7 fusion.87
  202.8 2.7 fusion.87
  209.6 2.7 fusion.87
  216.3 2.7 fusion.87
  224.2 2.6 collective-permute-start.1
  226.8 3.4 collective-permute-start.2
  233.4 2.9 collective-permute-start.6
  238.3 4.5 %collective-permute-done.4 = bf16[1,1,16384]{2,0,1:T(2,128)(2,1)S(1)} collective-permute-done((bf16[1,1,16384]{2,0,1:T(2,128)(2,1)S(1)}, bf16[1,1,16384]{2,0,1:T(2,128)(2,1)S(1)}, u32[]{:S(2)}, u32[]{:S(2)}) %collective-permute-start.4) | collective-permute-done | bytes 32800 | tf_op jit(solution)/shard_map/ppermute | solution.py:43
  245.1 4.2 collective-permute-start.11
  250.8 2.6 collective-permute-start.13
  272.7 2.4 convert_reduce_fusion.1
  276.0 2.7 bitcast_reduce_fusion
  278.7 58.0 %pmax.7 = f32[16,256]{1,0:T(8,128)S(1)} all-reduce(f32[16,256]{1,0:T(8,128)S(1)} %get-tuple-element.109), channel_id=1, replica_groups=mesh['scan'=2,'seq'=16] {'seq'}, use_global_device_ids=true, to_apply=%region_9.10 | all-reduce | flops 4096 | bytes 32768 | tf_op jit(solution)/shard_map/pmax | solution.py:181
  336.6 5.4 %fusion.45 = f32[16,64,256]{2,1,0:T(8,128)} fusion(bf16[256,16,64]{0,2,1:T(8,128)(2,1)S(1)} %bitcast.72, f32[16,256,256]{2,1,0:T(8,128)} %get-tuple-element.110, f32[16,256]{1,0:T(8,128)S(1)} %pmax.7), kind=kOutput, calls=%fused_computation.42 | convolution fusion | flops 807403520 | bytes 5783552 | tf_op jit(solution)/shard_map/hpn,nhd->phd/dot_general | solution.py:184
  342.1 2.9 fusion.44
  345.0 58.1 %psum.15 = f32[256,16]{0,1:T(8,128)S(1)} all-reduce(f32[256,16]{0,1:T(8,128)S(1)} %bitcast.82), channel_id=1, replica_groups=mesh['scan'=2,'seq'=16] {'seq'}, use_global_device_ids=true, to_apply=%region_12.13 | all-reduce | flops 4096 | bytes 32768 | tf_op jit(solution)/shard_map/psum | solution.py:187
  403.1 29.7 %all-reduce.2.cloned.1.call-done = f32[256,1024]{0,1:T(8,128)} async-done(((f32[256,1024]{0,1:T(8,128)}), f32[256,1024]{0,1:T(8,128)}) %all-reduce.2.cloned.1.call-update) | async-done | bytes 1048592 | tf_op jit(solution)/shard_map/psum | solution.py:187
  (143 shorter events, 69.4 us)
Async XLA Ops:
  7.2 151.4 %copy-start = (s32[32]{0:T(128)S(1)}, s32[32]{0:T(128)}, u32[]{:S(2)}) copy-start(s32[32]{0:T(128)} %param.21) | copy-start | bytes 388
  7.2 47.1 %all-gather.5.cloned.1.call-start = ((), (), s32[]{:S(2)}) async-start(), calls=%async_computation.2 | async-start | bytes 2228224 | tf_op jit(solution)/shard_map/all_gather | solution.py:84
  7.9 91.0 %all-gather.9.cloned.1.call-start = ((), (), s32[]{:S(2)}) async-start(), calls=%async_computation.4 | async-start | bytes 2228224 | tf_op jit(solution)/shard_map/all_gather | solution.py:94
  8.7 132.6 %all-gather.7.cloned.1.call-start = ((), (), s32[]{:S(2)}) async-start(), calls=%async_computation.3 | async-start | bytes 2228224 | tf_op jit(solution)/shard_map/all_gather | solution.py:89
  56.9 42.1 %copy-start.1 = (bf16[256,1024]{1,0:T(8,128)(2,1)S(1)}, bf16[256,1024]{1,0:T(8,128)(2,1)}, u32[]{:S(2)}) copy-start(bf16[256,1024]{1,0:T(8,128)(2,1)} %param.12) | copy-start | bytes 1572868
  56.9 42.1 %copy-start.7 = (f32[1024]{0:T(1024)S(1)}, f32[1024]{0:T(1024)}, u32[]{:S(2)}) copy-start(f32[1024]{0:T(1024)} %param.13) | copy-start | bytes 12292
  63.9 90.2 %all-to-all-start = ((bf16[16,2,8192]{2,1,0:T(2,128)(2,1)}), bf16[16,2,8192]{2,1,0:T(2,128)(2,1)}, u32[]{:S(2)}, u32[]{:S(2)}) async-start(bf16[16,2,8192]{2,1,0:T(2,128)(2,1)} %reshape.288), calls=%async_computation | async-start | bytes 1048576 | tf_op jit(solution)/shard_map/all_to_all | solution.py:112
  145.1 14.2 %copy-start.6 = (s32[32,8]{0,1:T(8,128)S(1)}, s32[32,8]{0,1:T(8,128)}, u32[]{:S(2)}) copy-start(s32[32,8]{0,1:T(8,128)} %param.20) | copy-start | bytes 3076
  154.1 29.3 %all-to-all-start.1 = ((bf16[16,2,16384]{2,1,0:T(2,128)(2,1)}), bf16[16,2,16384]{2,1,0:T(2,128)(2,1)S(1)}, u32[]{:S(2)}, u32[]{:S(2)}) async-start(bf16[16,2,16384]{2,1,0:T(2,128)(2,1)} %reshape.290), calls=%async_computation.1 | async-start | bytes 2097152 | tf_op jit(solution)/shard_map/all_to_all | solution.py:113
  157.7 115.0 %all-gather.11.cloned.1.call-start = ((), (), s32[]{:S(2)}) async-start(), calls=%async_computation.5 | async-start | bytes 2228224 | tf_op jit(solution)/shard_map/all_gather | solution.py:168
  158.3 274.4 %all-reduce.2.cloned.1.call-start = ((), (), s32[]{:S(2)}) async-start(), calls=%async_computation.6 | async-start | bytes 2097152 | tf_op jit(solution)/shard_map/psum | solution.py:187
  219.0 34.4 %copy-start.4 = (bf16[256,1024]{1,0:T(8,128)(2,1)S(1)}, bf16[256,1024]{1,0:T(8,128)(2,1)}, u32[]{:S(2)}) copy-start(bf16[256,1024]{1,0:T(8,128)(2,1)} %param.19) | copy-start | bytes 1572868
  221.4 51.3 %copy-start.2 = (bf16[256,1024]{1,0:T(8,128)(2,1)S(1)}, bf16[256,1024]{1,0:T(8,128)(2,1)}, u32[]{:S(2)}) copy-start(bf16[256,1024]{1,0:T(8,128)(2,1)} %param.12) | copy-start | bytes 1572868
  222.6 9.0 %collective-permute-start = (bf16[1,1,16384]{2,0,1:T(2,128)(2,1)S(1)}, bf16[1,1,16384]{2,0,1:T(2,128)(2,1)S(1)}, u32[]{:S(2)}, u32[]{:S(2)}) collective-permute-start(bf16[1,1,16384]{2,0,1:T(2,128)(2,1)S(1)} %get-tuple-element.106), channel_id=1, source_target_pairs={{0,1},{1,2},{2,3},{3,4},{4,5},{5,6},{6,7},{7,8},{8,9},{9,10},{10,1... | collective-permute-start | bytes 98312 | tf_op jit(solution)/shard_map/ppermute | solution.py:43
  224.2 9.2 %collective-permute-start.1 = (bf16[1,1,16384]{2,0,1:T(2,128)(2,1)S(1)}, bf16[1,1,16384]{2,0,1:T(2,128)(2,1)S(1)}, u32[]{:S(2)}, u32[]{:S(2)}) collective-permute-start(bf16[1,1,16384]{2,0,1:T(2,128)(2,1)S(1)} %get-tuple-element.105), channel_id=1, source_target_pairs={{0,2},{1,3},{2,4},{3,5},{4,6},{5,7},{6,8},{7,9},{8,10},{9,11},{10,... | collective-permute-start | bytes 98312 | tf_op jit(solution)/shard_map/ppermute | solution.py:43
  226.8 9.5 %collective-permute-start.2 = (bf16[1,1,16384]{2,0,1:T(2,128)(2,1)S(1)}, bf16[1,1,16384]{2,0,1:T(2,128)(2,1)S(1)}, u32[]{:S(2)}, u32[]{:S(2)}) collective-permute-start(bf16[1,1,16384]{2,0,1:T(2,128)(2,1)S(1)} %get-tuple-element.104), channel_id=1, source_target_pairs={{0,3},{1,4},{2,5},{3,6},{4,7},{5,8},{6,9},{7,10},{8,11},{9,12},{10... | collective-permute-start | bytes 98312 | tf_op jit(solution)/shard_map/ppermute | solution.py:43
  230.2 7.2 %collective-permute-start.3 = (bf16[1,1,16384]{2,0,1:T(2,128)(2,1)S(1)}, bf16[1,1,16384]{2,0,1:T(2,128)(2,1)S(1)}, u32[]{:S(2)}, u32[]{:S(2)}) collective-permute-start(bf16[1,1,16384]{2,0,1:T(2,128)(2,1)S(1)} %get-tuple-element.103), channel_id=1, source_target_pairs={{0,4},{1,5},{2,6},{3,7},{4,8},{5,9},{6,10},{7,11},{8,12},{9,13},{1... | collective-permute-start | bytes 98312 | tf_op jit(solution)/shard_map/ppermute | solution.py:43
  230.9 11.8 %collective-permute-start.4 = (bf16[1,1,16384]{2,0,1:T(2,128)(2,1)S(1)}, bf16[1,1,16384]{2,0,1:T(2,128)(2,1)S(1)}, u32[]{:S(2)}, u32[]{:S(2)}) collective-permute-start(bf16[1,1,16384]{2,0,1:T(2,128)(2,1)S(1)} %get-tuple-element.102), channel_id=1, source_target_pairs={{0,5},{1,6},{2,7},{3,8},{4,9},{5,10},{6,11},{7,12},{8,13},{9,14},{... | collective-permute-start | bytes 98312 | tf_op jit(solution)/shard_map/ppermute | solution.py:43
  231.5 13.6 %collective-permute-start.5 = (bf16[1,1,16384]{2,0,1:T(2,128)(2,1)S(1)}, bf16[1,1,16384]{2,0,1:T(2,128)(2,1)S(1)}, u32[]{:S(2)}, u32[]{:S(2)}) collective-permute-start(bf16[1,1,16384]{2,0,1:T(2,128)(2,1)S(1)} %get-tuple-element.101), channel_id=1, source_target_pairs={{0,6},{1,7},{2,8},{3,9},{4,10},{5,11},{6,12},{7,13},{8,14},{9,15},... | collective-permute-start | bytes 98312 | tf_op jit(solution)/shard_map/ppermute | solution.py:43
  233.4 11.7 %collective-permute-start.6 = (bf16[1,1,16384]{2,0,1:T(2,128)(2,1)S(1)}, bf16[1,1,16384]{2,0,1:T(2,128)(2,1)S(1)}, u32[]{:S(2)}, u32[]{:S(2)}) collective-permute-start(bf16[1,1,16384]{2,0,1:T(2,128)(2,1)S(1)} %get-tuple-element.100), channel_id=1, source_target_pairs={{0,7},{1,8},{2,9},{3,10},{4,11},{5,12},{6,13},{7,14},{8,15},{9,0},... | collective-permute-start | bytes 98312 | tf_op jit(solution)/shard_map/ppermute | solution.py:43
  236.3 13.0 %collective-permute-start.7 = (bf16[1,1,16384]{2,0,1:T(2,128)(2,1)S(1)}, bf16[1,1,16384]{2,0,1:T(2,128)(2,1)S(1)}, u32[]{:S(2)}, u32[]{:S(2)}) collective-permute-start(bf16[1,1,16384]{2,0,1:T(2,128)(2,1)S(1)} %get-tuple-element.99), channel_id=1, source_target_pairs={{0,8},{1,9},{2,10},{3,11},{4,12},{5,13},{6,14},{7,15},{8,0},{9,1},... | collective-permute-start | bytes 98312 | tf_op jit(solution)/shard_map/ppermute | solution.py:43
  237.3 13.5 %collective-permute-start.8 = (bf16[1,1,16384]{2,0,1:T(2,128)(2,1)S(1)}, bf16[1,1,16384]{2,0,1:T(2,128)(2,1)S(1)}, u32[]{:S(2)}, u32[]{:S(2)}) collective-permute-start(bf16[1,1,16384]{2,0,1:T(2,128)(2,1)S(1)} %get-tuple-element.98), channel_id=1, source_target_pairs={{0,9},{1,10},{2,11},{3,12},{4,13},{5,14},{6,15},{7,0},{8,1},{9,2},... | collective-permute-start | bytes 98312 | tf_op jit(solution)/shard_map/ppermute | solution.py:43
  242.8 10.6 %collective-permute-start.9 = (bf16[1,1,16384]{2,0,1:T(2,128)(2,1)S(1)}, bf16[1,1,16384]{2,0,1:T(2,128)(2,1)S(1)}, u32[]{:S(2)}, u32[]{:S(2)}) collective-permute-start(bf16[1,1,16384]{2,0,1:T(2,128)(2,1)S(1)} %get-tuple-element.97), channel_id=1, source_target_pairs={{0,10},{1,11},{2,12},{3,13},{4,14},{5,15},{6,0},{7,1},{8,2},{9,3},... | collective-permute-start | bytes 98312 | tf_op jit(solution)/shard_map/ppermute | solution.py:43
  245.1 20.3 %collective-permute-start.10 = (bf16[1,1,16384]{2,0,1:T(2,128)(2,1)S(1)}, bf16[1,1,16384]{2,0,1:T(2,128)(2,1)S(1)}, u32[]{:S(2)}, u32[]{:S(2)}) collective-permute-start(bf16[1,1,16384]{2,0,1:T(2,128)(2,1)S(1)} %get-tuple-element.96), channel_id=1, source_target_pairs={{0,11},{1,12},{2,13},{3,14},{4,15},{5,0},{6,1},{7,2},{8,3},{9,4},{... | collective-permute-start | bytes 98312 | tf_op jit(solution)/shard_map/ppermute | solution.py:43
  245.1 21.5 %collective-permute-start.11 = (bf16[1,1,16384]{2,0,1:T(2,128)(2,1)S(1)}, bf16[1,1,16384]{2,0,1:T(2,128)(2,1)S(1)}, u32[]{:S(2)}, u32[]{:S(2)}) collective-permute-start(bf16[1,1,16384]{2,0,1:T(2,128)(2,1)S(1)} %get-tuple-element.95), channel_id=1, source_target_pairs={{0,12},{1,13},{2,14},{3,15},{4,0},{5,1},{6,2},{7,3},{8,4},{9,5},{1... | collective-permute-start | bytes 98312 | tf_op jit(solution)/shard_map/ppermute | solution.py:43
  249.3 18.4 %collective-permute-start.12 = (bf16[1,1,16384]{2,0,1:T(2,128)(2,1)S(1)}, bf16[1,1,16384]{2,0,1:T(2,128)(2,1)S(1)}, u32[]{:S(2)}, u32[]{:S(2)}) collective-permute-start(bf16[1,1,16384]{2,0,1:T(2,128)(2,1)S(1)} %get-tuple-element.94), channel_id=1, source_target_pairs={{0,13},{1,14},{2,15},{3,0},{4,1},{5,2},{6,3},{7,4},{8,5},{9,6},{10... | collective-permute-start | bytes 98312 | tf_op jit(solution)/shard_map/ppermute | solution.py:43
  250.8 18.1 %collective-permute-start.13 = (bf16[1,1,16384]{2,0,1:T(2,128)(2,1)S(1)}, bf16[1,1,16384]{2,0,1:T(2,128)(2,1)S(1)}, u32[]{:S(2)}, u32[]{:S(2)}) collective-permute-start(bf16[1,1,16384]{2,0,1:T(2,128)(2,1)S(1)} %get-tuple-element.93), channel_id=1, source_target_pairs={{0,14},{1,15},{2,0},{3,1},{4,2},{5,3},{6,4},{7,5},{8,6},{9,7},{10,... | collective-permute-start | bytes 98312 | tf_op jit(solution)/shard_map/ppermute | solution.py:43
  253.4 16.6 %collective-permute-start.14 = (bf16[1,1,16384]{2,0,1:T(2,128)(2,1)S(1)}, bf16[1,1,16384]{2,0,1:T(2,128)(2,1)S(1)}, u32[]{:S(2)}, u32[]{:S(2)}) collective-permute-start(bf16[1,1,16384]{2,0,1:T(2,128)(2,1)S(1)} %get-tuple-element.92), channel_id=1, source_target_pairs={{0,15},{1,0},{2,1},{3,2},{4,3},{5,4},{6,5},{7,6},{8,7},{9,8},{10,9... | collective-permute-start | bytes 98312 | tf_op jit(solution)/shard_map/ppermute | solution.py:43
  261.9 13.5 %copy-start.5 = (f32[1024]{0:T(1024)S(1)}, f32[1024]{0:T(1024)}, u32[]{:S(2)}) copy-start(f32[1024]{0:T(1024)} %param.18) | copy-start | bytes 12292
  275.2 66.9 %copy-start.3 = (bf16[256,1024]{1,0:T(8,128)(2,1)}, bf16[256,1024]{1,0:T(8,128)(2,1)S(1)}, u32[]{:S(2)}) copy-start(bf16[256,1024]{1,0:T(8,128)(2,1)S(1)} %get-tuple-element.108) | copy-start | bytes 1572868
Sparse Core Ops, SparseCore 0:
  10.2 44.0 all-gather.4
  56.5 42.3 all-gather.8
  101.1 40.1 all-gather.6
  160.4 48.5 all-gather.10
  342.2 90.4 all-reduce.1
